TPU v7x, 128 devices: a whole 4x4x4 slice. The times are simulated.
128 devices in a mesh: row: 32 (over z_lo, x, y), pair: 4 (over z_hi, core).
Axes of the slice: x: 4, y: 4, z: 4 (z_hi: 2, z_lo: 2; z = z_hi * 2 + z_lo), core: 2. Of those that a mesh axis runs over, the one named last changes fastest.
Arguments:
- snapshots: float32 [512, 4, 16384], P('row', 'pair'), may hold values from -6 to 6
- plan: int32 [2, 8], replicated, may hold values from 0 to 7, each once within a row
Outputs:
- rotated: float32 [512, 4, 16384], P(None, 'pair', 'row')
Inputs may be any that keep to these rules, and one draw needn't show every extreme that they name: Each row of plan names every block once.
All inputs are finite; a program needn't handle non-finite values.
Results may differ from a plain program's by a relative error of at most 0.00013.
Values sent between devices are 32-bit elements; how exact they have to be, the bound alone decides.
A program may use at most 128 MiB of HBM per device.

v0:
```python
import jax
import jax.numpy as jnp
from jax import lax
from jax.sharding import PartitionSpec as P


def matmul(left, right):
    return jnp.dot(left, right, precision=lax.Precision.HIGHEST, preferred_element_type=jnp.float32)


def cayley(scaled):
    order_size = scaled.shape[0]
    identity = jnp.eye(order_size, dtype=jnp.float32)
    system = identity + matmul(scaled.T, scaled)
    lifted = identity + scaled
    square = matmul(lifted, lifted)
    lower = lax.linalg.cholesky(system)
    middle = lax.linalg.triangular_solve(lower, square, left_side=True, lower=True)
    return lax.linalg.triangular_solve(lower, middle, left_side=True, lower=True, transpose_a=True)


def locate(current, wanted):
    slot_ids = jnp.arange(current.shape[0], dtype=jnp.int32)
    hits = current[None, :] == wanted[:, None]
    return jnp.sum(jnp.where(hits, slot_ids[None, :], 0), axis=1)


def relocate(work, current, target):
    pair_here = lax.axis_index("pair")
    pair_total = lax.axis_size("pair")
    block_width = work.shape[0] // 2
    row_count = work.shape[1]
    wanted = lax.dynamic_slice_in_dim(target, 2 * pair_here, 2)
    positions = locate(current, wanted)
    everything = lax.all_gather(work, "pair", axis=0, tiled=True).reshape(
        2 * pair_total, block_width, row_count
    )
    upper_block = lax.dynamic_index_in_dim(everything, positions[0], 0, keepdims=False)
    lower_block = lax.dynamic_index_in_dim(everything, positions[1], 0, keepdims=False)
    return jnp.concatenate([upper_block, lower_block], axis=0)


def rotate_whole(work):
    order_size = work.shape[0]
    gram = lax.psum(matmul(work, work.T), "row")
    scales = lax.rsqrt(jnp.diagonal(gram))
    normed = gram * scales[:, None] * scales[None, :]
    column_ids = jnp.arange(order_size, dtype=jnp.int32)
    signs = jnp.sign(column_ids[None, :] - column_ids[:, None]).astype(jnp.float32)
    skew = normed * signs
    factor = 1.0 + jnp.sqrt(jnp.sum(skew * skew))
    turn = cayley(skew / factor)
    return matmul(turn.T, work)


def on_device(snapshots, plan):
    arrived = lax.all_to_all(snapshots, "row", split_axis=2, concat_axis=0, tiled=True)
    work = arrived[:, 0, :]
    block_total = plan.shape[1]
    natural_order = jnp.arange(block_total, dtype=jnp.int32)
    current = natural_order
    for round_index in range(plan.shape[0]):
        target = plan[round_index]
        work = relocate(work, current, target)
        current = target
        work = rotate_whole(work)
    work = relocate(work, current, natural_order)
    return work[:, None, :]


def solution(mesh):
    in_specs = (P("row", "pair", None), P())
    out_specs = P(None, "pair", "row")
    return jax.shard_map(
        on_device, mesh=mesh, in_specs=in_specs, out_specs=out_specs, check_vma=False
    )
```

profile of v0, /device:TPU:1, one launch (start us, length us, event | category | flops | bytes accessed | tf_op | source)
XLA Modules:
  0.0 1240.9 jit_solution(9342640069578683527)
XLA Ops:
  6.5 15.5 %copy.30 = f32[16,1,16384]{0,1,2:T(1,128)} copy(f32[16,1,16384]{2,1,0:T(1,128)} %param.7) | data formatting | bytes 2097152 | tf_op args[0]
  22.6 74.5 %reduce.96 = f32[16384,16]{1,0:T(8,128)} reduce(f32[16384,1,16]{2,1,0:T(1,128)} %bitcast.161, f32[]{:T(128)} %broadcast.231), dimensions={1}, to_apply=%bitcast.125.reduce_sub_computation | reduce | bytes 2097156
  97.0 6.1 reshape.185
  103.1 24.7 %all_to_all.15 = f32[32,1,8192]{2,1,0:T(1,128)S(1)} all-to-all(f32[32,1,8192]{2,1,0:T(1,128)S(1)} %reshape.185), channel_id=1, replica_groups=mesh['row'=32,'pair'=4] {'row'}, dimensions={0} | all-to-all | bytes 2097152 | tf_op jit(solution)/shard_map/all_to_all | solution.py:57
  131.1 17.3 %reshape.186 = f32[16384,1,16]{2,1,0:T(1,128)} reshape(f32[32,8192]{1,0:T(8,128)S(1)} %reduce.97) | data formatting | bytes 2097152
  148.3 5.3 copy.37
  160.7 34.6 %all-gather.4.cloned.1.call-done = f32[2048,512]{1,0:T(8,128)} async-done(((f32[512,512]{1,0:T(8,128)}), f32[2048,512]{1,0:T(8,128)}) %all-gather.4.cloned.1.call-update) | async-done | bytes 4194320 | tf_op jit(solution)/shard_map/all_gather | solution.py:35
  201.1 287.3 %all-reduce.4.cloned.1.call-done = f32[512,512]{1,0:T(8,128)} async-done(((f32[512,512]{1,0:T(8,128)}), f32[512,512]{1,0:T(8,128)}) %all-reduce.4.cloned.1.call-update) | async-done | bytes 1048592 | tf_op jit(solution)/shard_map/psum | solution.py:45
  488.4 8.6 gather_fusion
  499.9 3.9 fusion.139
  504.4 11.7 custom-call.43
  516.7 9.8 custom-call.44
  527.6 12.7 %custom-call.45 = f32[128,128]{1,0:T(8,128)} custom-call(f32[128,128]{1,0:T(8,128)S(1)} %slice.298), custom_call_target="Cholesky" | custom-call | tf_op jit(solution)/shard_map/cholesky/custom-call.5 | solution.py:17
  542.8 9.8 custom-call.46
  553.2 11.7 custom-call.47
  565.0 9.8 custom-call.48
  575.4 11.9 custom-call.49
  593.8 7.9 while.8
  601.7 39.3 %custom-call.51 = f32[4,128,128]{1,2,0:T(8,128)S(1)} custom-call(f32[4,128,128]{2,1,0:T(8,128)S(1)} %get-tuple-element.37), custom_call_target="InvertDiagBlocksLowerTriangular" | custom-call | tf_op jit(solution)/shard_map/triangular_solve/custom-call.8 | solution.py:19
  657.1 57.0 %all-gather.6.cloned.1.call-done = f32[2048,512]{1,0:T(8,128)} async-done(((f32[512,512]{1,0:T(8,128)}), f32[2048,512]{1,0:T(8,128)}) %all-gather.6.cloned.1.call-update) | async-done | bytes 4194320 | tf_op jit(solution)/shard_map/all_gather | solution.py:35
  719.3 287.8 %all-reduce.6.cloned.1.call-done = f32[512,512]{1,0:T(8,128)} async-done(((f32[512,512]{1,0:T(8,128)}), f32[512,512]{1,0:T(8,128)}) %all-reduce.6.cloned.1.call-update) | async-done | bytes 1048592 | tf_op jit(solution)/shard_map/psum | solution.py:45
  1007.2 8.8 gather_fusion.1
  1023.4 11.7 custom-call.52
  1035.7 9.8 custom-call.53
  1046.6 12.5 %custom-call.54 = f32[128,128]{1,0:T(8,128)} custom-call(f32[128,128]{1,0:T(8,128)S(1)} %slice.325), custom_call_target="Cholesky" | custom-call | tf_op jit(solution)/shard_map/cholesky/custom-call.5 | solution.py:17
  1061.0 9.8 custom-call.55
  1071.5 11.7 custom-call.56
  1083.2 9.8 custom-call.57
  1093.6 11.9 custom-call.58
  1110.8 7.9 while.9
  1118.7 39.3 %custom-call.60 = f32[4,128,128]{1,2,0:T(8,128)S(1)} custom-call(f32[4,128,128]{2,1,0:T(8,128)S(1)} %get-tuple-element.39), custom_call_target="InvertDiagBlocksLowerTriangular" | custom-call | tf_op jit(solution)/shard_map/triangular_solve/custom-call.8 | solution.py:19
  1174.1 57.0 %all-gather.8.cloned.1.call-done = f32[2048,512]{1,0:T(8,128)} async-done(((f32[512,512]{1,0:T(8,128)}), f32[2048,512]{1,0:T(8,128)}) %all-gather.8.cloned.1.call-update) | async-done | bytes 4194320 | tf_op jit(solution)/shard_map/all_gather | solution.py:35
  (170 shorter events, 86.9 us)
Async XLA Ops:
  6.5 188.8 %all-gather.4.cloned.1.call-start = ((), (), s32[]{:S(2)}) async-start(), calls=%async_computation.1 | async-start | bytes 5242880 | tf_op jit(solution)/shard_map/all_gather | solution.py:35
  148.3 6.9 copy-start.12
  155.2 333.2 %all-reduce.4.cloned.1.call-start = ((), (), s32[]{:S(2)}) async-start(), calls=%async_computation.2 | async-start | bytes 2097152 | tf_op jit(solution)/shard_map/psum | solution.py:45
  196.6 0.8 copy-start.6
  196.6 1.0 copy-start.8
  200.5 513.6 %all-gather.6.cloned.1.call-start = ((), (), s32[]{:S(2)}) async-start(), calls=%async_computation.3 | async-start | bytes 5242880 | tf_op jit(solution)/shard_map/all_gather | solution.py:35
  516.1 0.6 copy-start.10
  526.5 114.5 %copy-start.1 = (f32[512,512]{1,0:T(8,128)S(1)}, f32[512,512]{1,0:T(8,128)}, u32[]{:S(2)}) copy-start(f32[512,512]{1,0:T(8,128)} %all-reduce.4.cloned.1.call-done) | copy-start | bytes 3145732
  645.0 4.6 copy-start.7
  645.0 4.6 copy-start.9
  652.5 354.7 %all-reduce.6.cloned.1.call-start = ((), (), s32[]{:S(2)}) async-start(), calls=%async_computation.4 | async-start | bytes 2097152 | tf_op jit(solution)/shard_map/psum | solution.py:45
  715.4 0.8 copy-start.2
  715.4 1.0 copy-start.4
  719.3 511.9 %all-gather.8.cloned.1.call-start = ((), (), s32[]{:S(2)}) async-start(), calls=%async_computation.5 | async-start | bytes 5242880 | tf_op jit(solution)/shard_map/all_gather | solution.py:35
  1035.1 0.6 copy-start.11
  1045.5 112.5 %copy-start = (f32[512,512]{1,0:T(8,128)S(1)}, f32[512,512]{1,0:T(8,128)}, u32[]{:S(2)}) copy-start(f32[512,512]{1,0:T(8,128)} %all-reduce.6.cloned.1.call-done) | copy-start | bytes 3145732
  1162.0 4.6 copy-start.3
  1162.0 4.6 copy-start.5
  1164.7 4.9 copy-start.13
Sparse Core Ops, SparseCore 0:
  155.3 39.9 all-gather.3
  200.6 287.7 all-reduce.3
  652.6 61.4 all-gather.5
  719.4 287.7 all-reduce.5
  1169.6 61.4 all-gather.7
where the time goes:
time: 1250 us; the launch traced here: 1240 us
  waiting for transfers between devices  724 us (58%)
  other arithmetic  325 us (26%)
  local copies, waits for them, and re-layouts  94.2 us (8%)
  matrix products  40.3 us (3%)
  between operations  32 us (3%)
  blocking collectives  24.7 us (2%)
    psum x2, waiting for transfers between devices, rotate_whole(): gram = lax.psum(matmul(work, work.T), 'row')  575 us
    another operation x30, other arithmetic, cayley(): lower = lax.linalg.cholesky(system)  163 us
    all_gather x3, waiting for transfers between devices, relocate(): lax.all_gather(work, 'pair', axis=0, tiled=True)  149 us
    another operation x5, other arithmetic, cayley(): lax.linalg.triangular_solve(lower, middle, left_side=True, lower=True, tr...  79.4 us
    unnamed x1, other arithmetic  74.5 us
    unnamed x32, local copies, waits for them, and re-layouts  42.6 us
  transfers between devices with their start and end apart: 5, of which 5 were waited for; matrix products, arithmetic and copies ran while one was open for 0% of the time, Pallas kernels for 0%

commit v1 on v0

--- a/solution.py
+++ b/solution.py
@@ -42,7 +42,7 @@
 
 def rotate_whole(work):
     order_size = work.shape[0]
-    gram = lax.psum(matmul(work, work.T), "row")
+    gram = jnp.sum(lax.all_gather(matmul(work, work.T), "row"), axis=0)
     scales = lax.rsqrt(jnp.diagonal(gram))
     normed = gram * scales[:, None] * scales[None, :]
     column_ids = jnp.arange(order_size, dtype=jnp.int32)

time: 1250 us -> 1360 us (1.088)
  waiting for transfers between devices: 724 us -> 825 us
  other arithmetic: 325 us -> 343 us
    all_gather x0 -> x2, waiting for transfers between devices: none -> 727 us  [rotate_whole(): gram = jnp.sum(lax.all_gather(matmul(work, work.T), 'row'), axis=0)]
    psum x2 -> x0, waiting for transfers between devices: 575 us -> none  [rotate_whole(): gram = lax.psum(matmul(work, work.T), 'row')]
    all_gather x3, waiting for transfers between devices: 149 us -> 98.4 us  [relocate(): lax.all_gather(work, 'pair', axis=0, tiled=True)]
    reduce_sum x0 -> x2, other arithmetic: none -> 24.6 us  [rotate_whole(): gram = jnp.sum(lax.all_gather(matmul(work, work.T), 'row'), axis=0)]
    unnamed x32 -> x22, local copies, waits for them, and re-layouts: 42.6 us -> 41.3 us
where the time goes in v1:
time: 1360 us
  waiting for transfers between devices  825 us (61%)
  other arithmetic  343 us (25%)
  local copies, waits for them, and re-layouts  83.3 us (6%)
  matrix products  46.8 us (3%)
  between operations  31.6 us (2%)
  blocking collectives  24.6 us (2%)
    all_gather x2, waiting for transfers between devices, rotate_whole(): gram = jnp.sum(lax.all_gather(matmul(work, work.T), 'row'), axis=0)  727 us
    another operation x30, other arithmetic, cayley(): lower = lax.linalg.cholesky(system)  159 us
    all_gather x3, waiting for transfers between devices, relocate(): lax.all_gather(work, 'pair', axis=0, tiled=True)  98.4 us
    another operation x5, other arithmetic, cayley(): lax.linalg.triangular_solve(lower, middle, left_side=True, lower=True, tr...  79.5 us
    unnamed x1, other arithmetic  74.5 us
    unnamed x22, local copies, waits for them, and re-layouts  41.3 us
  transfers between devices with their start and end apart: 5, of which 5 were waited for; matrix products, arithmetic and copies ran while one was open for 0% of the time, Pallas kernels for 0%

profile of v1, /device:TPU:1, one launch (start us, length us, event | category | flops | bytes accessed | tf_op | source)
XLA Modules:
  0.0 1355.3 jit_solution(11180873061655975761)
XLA Ops:
  6.5 15.5 %copy.30 = f32[16,1,16384]{0,1,2:T(1,128)} copy(f32[16,1,16384]{2,1,0:T(1,128)} %param.7) | data formatting | bytes 2097152 | tf_op args[0]
  22.6 74.5 %reduce.96 = f32[16384,16]{1,0:T(8,128)} reduce(f32[16384,1,16]{2,1,0:T(1,128)} %bitcast.163, f32[]{:T(128)} %broadcast.231), dimensions={1}, to_apply=%bitcast.127.reduce_sub_computation | reduce | bytes 2097156
  97.0 6.1 reshape.187
  103.1 24.6 %all_to_all.15 = f32[32,1,8192]{2,1,0:T(1,128)S(1)} all-to-all(f32[32,1,8192]{2,1,0:T(1,128)S(1)} %reshape.187), channel_id=1, replica_groups=mesh['row'=32,'pair'=4] {'row'}, dimensions={0} | all-to-all | bytes 2097152 | tf_op jit(solution)/shard_map/all_to_all | solution.py:57
  130.9 17.3 %reshape.188 = f32[16384,1,16]{2,1,0:T(1,128)} reshape(f32[32,8192]{1,0:T(8,128)S(1)} %reduce.97) | data formatting | bytes 2097152
  148.2 5.3 copy.37
  159.8 35.4 %all-gather.8.cloned.1.call-done = f32[2048,512]{1,0:T(8,128)} async-done(((f32[512,512]{1,0:T(8,128)}), f32[2048,512]{1,0:T(8,128)}) %all-gather.8.cloned.1.call-update) | async-done | bytes 4194320 | tf_op jit(solution)/shard_map/all_gather | solution.py:35
  200.4 363.4 %all-gather.14.cloned.1.call-done = f32[16384,512]{1,0:T(8,128)} async-done(((f32[512,512]{1,0:T(8,128)}), f32[16384,512]{1,0:T(8,128)}) %all-gather.14.cloned.1.call-update) | async-done | bytes 33554448 | tf_op jit(solution)/shard_map/all_gather | solution.py:45
  563.8 12.3 reduce_sum.64
  576.0 5.0 gather_fusion
  589.0 11.7 custom-call.43
  600.9 9.8 custom-call.44
  612.0 11.7 custom-call.45
  625.1 9.8 custom-call.46
  635.5 11.7 custom-call.47
  648.0 10.0 custom-call.48
  658.6 11.7 custom-call.49
  673.7 8.1 while.8
  681.9 39.7 %custom-call.51 = f32[4,128,128]{1,2,0:T(8,128)S(1)} custom-call(f32[4,128,128]{2,1,0:T(8,128)S(1)} %get-tuple-element.37), custom_call_target="InvertDiagBlocksLowerTriangular" | custom-call | tf_op jit(solution)/shard_map/triangular_solve/custom-call.8 | solution.py:19
  738.9 31.6 %all-gather.10.cloned.1.call-done = f32[2048,512]{1,0:T(8,128)} async-done(((f32[512,512]{1,0:T(8,128)}), f32[2048,512]{1,0:T(8,128)}) %all-gather.10.cloned.1.call-update) | async-done | bytes 4194320 | tf_op jit(solution)/shard_map/all_gather | solution.py:35
  775.7 363.4 %all-gather.16.cloned.1.call-done = f32[16384,512]{1,0:T(8,128)} async-done(((f32[512,512]{1,0:T(8,128)}), f32[16384,512]{1,0:T(8,128)}) %all-gather.16.cloned.1.call-update) | async-done | bytes 33554448 | tf_op jit(solution)/shard_map/all_gather | solution.py:45
  1139.1 12.3 reduce_sum.67
  1164.0 11.7 custom-call.52
  1175.9 9.8 custom-call.53
  1187.0 11.7 custom-call.54
  1200.1 9.8 custom-call.55
  1210.6 11.7 custom-call.56
  1223.0 10.2 custom-call.57
  1233.8 11.7 custom-call.58
  1249.0 8.1 while.9
  1257.1 39.5 %custom-call.60 = f32[4,128,128]{1,2,0:T(8,128)S(1)} custom-call(f32[4,128,128]{2,1,0:T(8,128)S(1)} %get-tuple-element.39), custom_call_target="InvertDiagBlocksLowerTriangular" | custom-call | tf_op jit(solution)/shard_map/triangular_solve/custom-call.8 | solution.py:19
  1314.2 31.4 %all-gather.12.cloned.1.call-done = f32[2048,512]{1,0:T(8,128)} async-done(((f32[512,512]{1,0:T(8,128)}), f32[2048,512]{1,0:T(8,128)}) %all-gather.12.cloned.1.call-update) | async-done | bytes 4194320 | tf_op jit(solution)/shard_map/all_gather | solution.py:35
  (162 shorter events, 93.3 us)
Async XLA Ops:
  6.5 188.6 %all-gather.8.cloned.1.call-start = ((), (), s32[]{:S(2)}) async-start(), calls=%async_computation.1 | async-start | bytes 5242880 | tf_op jit(solution)/shard_map/all_gather | solution.py:35
  148.2 6.9 copy-start.8
  155.0 408.7 %all-gather.14.cloned.1.call-start = ((), (), s32[]{:S(2)}) async-start(), calls=%async_computation.4 | async-start | bytes 34603008 | tf_op jit(solution)/shard_map/all_gather | solution.py:45
  196.4 0.8 copy-start.4
  196.4 1.0 copy-start.6
  200.3 570.3 %all-gather.10.cloned.1.call-start = ((), (), s32[]{:S(2)}) async-start(), calls=%async_computation.2 | async-start | bytes 5242880 | tf_op jit(solution)/shard_map/all_gather | solution.py:35
  726.1 5.5 copy-start.5
  726.1 5.5 copy-start.7
  734.6 404.5 %all-gather.16.cloned.1.call-start = ((), (), s32[]{:S(2)}) async-start(), calls=%async_computation.5 | async-start | bytes 34603008 | tf_op jit(solution)/shard_map/all_gather | solution.py:45
  771.8 0.8 copy-start
  771.8 1.0 copy-start.2
  775.6 569.9 %all-gather.12.cloned.1.call-start = ((), (), s32[]{:S(2)}) async-start(), calls=%async_computation.3 | async-start | bytes 5242880 | tf_op jit(solution)/shard_map/all_gather | solution.py:35
  1301.1 5.5 copy-start.1
  1301.1 5.5 copy-start.3
Sparse Core Ops, SparseCore 0:
  155.1 39.9 all-gather.7
  200.4 363.3 all-gather.13
  734.7 35.7 all-gather.9
  775.8 363.3 all-gather.15
  1309.7 35.7 all-gather.11
